TPU v7x, 128 devices: a whole 4x4x4 slice. The times are simulated.
128 devices in a mesh: dp: 2 (over z_lo), head: 8 (over z_hi, y), tensor: 8 (over x, core).
Axes of the slice: x: 4, y: 4, z: 4 (z_hi: 2, z_lo: 2; z = z_hi * 2 + z_lo), core: 2. Of those that a mesh axis runs over, the one named last changes fastest.
Arguments:
- tokens: bfloat16 [512, 8192], P('dp', 'tensor'), may hold values from -6 to 6
- cotangent: bfloat16 [512, 8192], P('dp', 'tensor'), may hold values from -6 to 6
- w_gate: bfloat16 [8192, 29568], P('tensor', 'head'), may hold values from -0.0625 to 0.0625
- w_up: bfloat16 [8192, 29568], P('tensor', 'head'), may hold values from -0.0625 to 0.0625
- w_down: bfloat16 [29568, 8192], P('head', 'tensor'), may hold values from -0.03125 to 0.03125
- common_down_factor: bfloat16 [8192, 64], P('tensor'), may hold values from -0.0625 to 0.0625
- head_up: bfloat16 [64, 64, 8192], P('head', None, 'tensor'), may hold values from -0.0625 to 0.0625
- routes: int32 [512, 1], P('dp'), may hold values from 0 to 63
Outputs:
- grad_x: bfloat16 [512, 8192], P(('dp', 'head'), 'tensor')
- grad_shared: float32 [8192, 64], P('tensor')
- up_head_gradients: float32 [64, 64, 8192], P('head', None, 'tensor')
Inputs may be any that keep to these rules, and one draw needn't show every extreme that they name: `routes`: each token names one adapter head; the loads are skewed.
All inputs are finite; a program needn't handle non-finite values.
Results may differ from a plain program's by a relative error of at most 0.015.
Values may be sent and summed in bfloat16 or wider, within the bound.
A program may use at most 128 MiB of HBM per device.

v0:
```python
import jax
import jax.numpy as jnp
from jax import lax
from jax.sharding import PartitionSpec as P

ADAPTER_SCALE = 2.0


def contract_last(left, right):
    return lax.dot_general(
        left, right, (((1,), (1,)), ((), ())), preferred_element_type=jnp.float32
    )


def local(tokens, cotangent, w_gate, w_up, w_down, common_down_factor, head_up, routes):
    tok_rows, d_cols = tokens.shape
    hidden_activation = w_gate.shape[1]
    reduced_activation = common_down_factor.shape[1]
    local_heads = head_up.shape[0]
    first_head = lax.axis_index("head") * local_heads
    assigned_mask = (
        routes == first_head + jnp.arange(local_heads, dtype=jnp.int32)[None, :]
    ).astype(jnp.float32)
    flat_heads = head_up.reshape(local_heads * reduced_activation, d_cols)
    gate_preactivation = jnp.dot(tokens, w_gate, preferred_element_type=jnp.float32)
    up_preactivation = jnp.dot(tokens, w_up, preferred_element_type=jnp.float32)
    returned_gradient = contract_last(cotangent, w_down)
    adapter_selectors = jnp.dot(tokens, common_down_factor, preferred_element_type=jnp.float32)
    head_separated = contract_last(cotangent, flat_heads).reshape(
        tok_rows, local_heads, reduced_activation
    )
    selector_gradient = ADAPTER_SCALE * jnp.sum(head_separated * assigned_mask[:, :, None], axis=1)
    combined_total = lax.psum(
        jnp.concatenate(
            [
                gate_preactivation,
                up_preactivation,
                returned_gradient,
                adapter_selectors,
                selector_gradient,
            ],
            axis=1,
        ),
        "tensor",
    )
    gate_preactivation = combined_total[:, :hidden_activation]
    up_preactivation = combined_total[:, hidden_activation : 2 * hidden_activation]
    returned_gradient = combined_total[:, 2 * hidden_activation : 3 * hidden_activation]
    adapter_selectors = combined_total[
        :, 3 * hidden_activation : 3 * hidden_activation + reduced_activation
    ].astype(jnp.bfloat16)
    selector_gradient = combined_total[:, 3 * hidden_activation + reduced_activation :].astype(
        jnp.bfloat16
    )
    sig_gate = jax.nn.sigmoid(gate_preactivation)
    gate_gradient = (
        returned_gradient
        * up_preactivation
        * sig_gate
        * (1.0 + gate_preactivation * (1.0 - sig_gate))
    ).astype(jnp.bfloat16)
    up_gradient = (returned_gradient * gate_preactivation * sig_gate).astype(jnp.bfloat16)
    gate_gradient, up_gradient, adapter_selectors, selector_gradient = (
        gate_gradient,
        up_gradient,
        adapter_selectors,
        selector_gradient,
    )
    ffn_part = contract_last(gate_gradient, w_gate) + contract_last(up_gradient, w_up)
    own_ffn, own_code = (
        lax.psum_scatter(ffn_part, "head", scatter_dimension=0, tiled=True),
        lax.psum_scatter(
            selector_gradient.astype(jnp.float32), "head", scatter_dimension=0, tiled=True
        ),
    )
    grad_x = (own_ffn + contract_last(own_code.astype(jnp.bfloat16), common_down_factor)).astype(
        jnp.bfloat16
    )
    selector_mask = (
        adapter_selectors[:, None, :] * assigned_mask[:, :, None].astype(jnp.bfloat16)
    ).reshape(tok_rows, local_heads * reduced_activation)
    head_contributions = ADAPTER_SCALE * lax.dot_general(
        selector_mask, cotangent, (((0,), (0,)), ((), ())), preferred_element_type=jnp.float32
    )
    up_head_gradients = lax.psum(
        head_contributions.reshape(local_heads, reduced_activation, d_cols).astype(jnp.bfloat16),
        "dp",
    ).astype(jnp.float32)
    shared_term = lax.dot_general(
        tokens, selector_gradient, (((0,), (0,)), ((), ())), preferred_element_type=jnp.float32
    )
    grad_shared = lax.psum(shared_term.astype(jnp.bfloat16), ("dp", "head")).astype(jnp.float32)
    return (grad_x, grad_shared, up_head_gradients)


def solution(mesh):
    placed = (
        P("dp", "tensor"),
        P("dp", "tensor"),
        P("tensor", "head"),
        P("tensor", "head"),
        P("head", "tensor"),
        P("tensor", None),
        P("head", None, "tensor"),
        P("dp", None),
    )
    return jax.shard_map(
        local,
        mesh=mesh,
        in_specs=placed,
        out_specs=(P(("dp", "head"), "tensor"), P("tensor", None), P("head", None, "tensor")),
        check_vma=False,
    )
```

profile of v0, /device:TPU:0, one launch (start us, length us, event | category | flops | bytes accessed | tf_op | source)
XLA Modules:
  0.0 459.9 jit_solution(7197060639671306123)
XLA Ops:
  7.3 0.9 fusion.15
  8.2 7.9 %convolution_dynamic-update-slice_fusion.2 = f32[256,11216]{0,1:T(8,128)} fusion(bf16[256,1024]{1,0:T(8,128)(2,1)} %param.8, bf16[1024,3696]{0,1:T(8,128)(2,1)} %param.10), kind=kOutput, calls=%fused_computation.2 | convolution fusion | flops 1937768448 | bytes 11878400 | tf_op jit(solution)/shard_map/dot_general | solution.py:25
  16.1 4.3 convolution_dynamic-update-slice_fusion.1
  20.4 0.5 fusion.9
  20.9 4.3 convolution_dynamic-update-slice_fusion
  25.2 0.9 convolution_dynamic-update-slice_fusion.3
  26.1 0.6 multiply_dynamic-update-slice_fusion
  26.8 135.7 %all-reduce.4.cloned.1.call-done = f32[256,11216]{0,1:T(8,128)} async-done(((f32[256,11216]{0,1:T(8,128)}), f32[256,11216]{0,1:T(8,128)}) %all-reduce.4.cloned.1.call-update) | async-done | bytes 11485200 | tf_op jit(solution)/shard_map/psum | solution.py:33
  162.5 4.8 %convert.4 = bf16[256,11216]{0,1:T(8,128)(2,1)S(1)} convert(f32[256,11216]{0,1:T(8,128)} %all-reduce.4.cloned.1.call-done) | non-fusion elementwise | flops 2871296 | bytes 17227776 | tf_op jit(solution)/shard_map/convert.1
  167.4 2.4 copy-done.1
  169.8 0.9 fusion.10
  170.7 0.8 fusion.18
  171.5 0.8 copy.13
  172.4 1.4 multiply_convert_fusion.1
  174.1 7.7 %fusion.3 = f32[256,1024]{1,0:T(8,128)S(1)} fusion(bf16[1024,3696]{0,1:T(8,128)(2,1)} %param.11, f32[256,11216]{0,1:T(8,128)} %all-reduce.4.cloned.1.call-done), kind=kOutput, calls=%fused_computation.10 | convolution fusion | flops 1943445504 | bytes 16187392 | tf_op jit(solution)/shard_map/dot_general | solution.py:10
  181.7 10.2 %fusion.6 = f32[256,1024]{1,0:T(8,128)} fusion(f32[256,1024]{1,0:T(8,128)S(1)} %fusion.3, bf16[1024,3696]{0,1:T(8,128)(2,1)} %param.10, f32[256,11216]{0,1:T(8,128)} %all-reduce.4.cloned.1.call-done), kind=kOutput, calls=%fused_computation.12 | convolution fusion | flops 1947492352 | bytes 21020672 | tf_op jit(solution)/shard_map/dot_general | solution.py:10
  192.0 61.1 %all-reduce.6.cloned.1.call-done = bf16[1024,64]{0,1:T(8,128)(2,1)} async-done(((bf16[1024,64]{0,1:T(8,128)(2,1)}), bf16[1024,64]{0,1:T(8,128)(2,1)}) %all-reduce.6.cloned.1.call-update) | async-done | bytes 131088 | tf_op jit(solution)/shard_map/psum | solution.py:92
  253.1 1.6 convert_element_type.61
  254.7 71.5 %reduce-scatter.7.cloned.1.call-done = f32[32,64]{1,0:T(8,128)} async-done(((f32[256,64]{1,0:T(8,128)}), f32[32,64]{1,0:T(8,128)}) %reduce-scatter.7.cloned.1.call-update) | async-done | bytes 8208
  326.2 0.8 copy.14
  327.0 48.0 %all-reduce.8.cloned.1.call-done = bf16[8,64,1024]{2,1,0:T(8,128)(2,1)} async-done(((bf16[8,64,1024]{2,1,0:T(8,128)(2,1)}), bf16[8,64,1024]{2,1,0:T(8,128)(2,1)}) %all-reduce.8.cloned.1.call-update) | async-done | bytes 1048592 | tf_op jit(solution)/shard_map/psum | solution.py:85
  375.0 2.8 convert_element_type.65
  377.8 73.9 %reduce-scatter.5.cloned.1.call-done = f32[32,1024]{1,0:T(8,128)} async-done(((f32[256,1024]{1,0:T(8,128)}), f32[32,1024]{1,0:T(8,128)}) %reduce-scatter.5.cloned.1.call-update) | async-done | bytes 131088 | tf_op jit(solution)/shard_map/reduce_scatter | solution.py:71
  451.7 1.7 fusion.11
  (28 shorter events, 0.5 us)
Async XLA Ops:
  7.2 13.2 %copy-start = (bf16[8,64,1024]{2,1,0:T(8,128)(2,1)S(1)}, bf16[8,64,1024]{2,1,0:T(8,128)(2,1)}, u32[]{:S(2)}) copy-start(bf16[8,64,1024]{2,1,0:T(8,128)(2,1)} %param.14) | copy-start | bytes 3145732
  7.2 8.9 %copy-start.2 = (bf16[256,1024]{1,0:T(8,128)(2,1)S(1)}, bf16[256,1024]{1,0:T(8,128)(2,1)}, u32[]{:S(2)}) copy-start(bf16[256,1024]{1,0:T(8,128)(2,1)} %param.8) | copy-start | bytes 1572868
  7.2 155.3 %all-reduce.4.cloned.1.call-start = ((), (), s32[]{:S(2)}) async-start(), calls=%async_computation.2 | async-start | bytes 22970368 | tf_op jit(solution)/shard_map/psum | solution.py:33
  7.2 8.8 %copy-start.5 = (bf16[1024,3696]{0,1:T(8,128)(2,1)S(1)}, bf16[1024,3696]{0,1:T(8,128)(2,1)}, u32[]{:S(2)}) copy-start(bf16[1024,3696]{0,1:T(8,128)(2,1)} %param.11) | copy-start | bytes 22708228
  8.2 12.7 %slice-start = ((s8[7569408]{0:T(1024)(128)(4,1)}), s8[4194304]{0:T(1024)(128)(4,1)S(1)}, s32[]{:S(2)}) async-start(s8[7569408]{0:T(1024)(128)(4,1)} %bitcast.28), calls=%async_computation.7 | async-start | bytes 8388608
  16.1 4.3 copy-start.3
  16.1 4.8 %slice-start.1 = ((s8[7569408]{0:T(1024)(128)(4,1)}), s8[3375104]{0:T(1024)(128)(4,1)S(1)}, s32[]{:S(2)}) async-start(s8[7569408]{0:T(1024)(128)(4,1)} %bitcast.28), calls=%async_computation.8 | async-start | bytes 6750208
  20.4 4.8 %copy-start.4 = (bf16[1024,64]{0,1:T(8,128)(2,1)S(1)}, bf16[1024,64]{0,1:T(8,128)(2,1)}, u32[]{:S(2)}) copy-start(bf16[1024,64]{0,1:T(8,128)(2,1)} %param.13) | copy-start | bytes 393220
  26.8 226.4 %all-reduce.6.cloned.1.call-start = ((), (), s32[]{:S(2)}) async-start(), calls=%async_computation.4 | async-start | bytes 262144 | tf_op jit(solution)/shard_map/psum | solution.py:92
  167.4 2.5 copy-start.1
  170.7 155.5 %reduce-scatter.7.cloned.1.call-start = ((), (), s32[]{:S(2)}) async-start(), calls=%async_computation.6 | async-start | bytes 147456
  172.3 202.7 %all-reduce.8.cloned.1.call-start = ((), (), s32[]{:S(2)}) async-start(), calls=%async_computation.5 | async-start | bytes 2097152 | tf_op jit(solution)/shard_map/psum | solution.py:85
  173.8 277.9 %reduce-scatter.5.cloned.1.call-start = ((), (), s32[]{:S(2)}) async-start(), calls=%async_computation.3 | async-start | bytes 1179648 | tf_op jit(solution)/shard_map/reduce_scatter | solution.py:71
Sparse Core Ops, SparseCore 0:
  26.9 135.6 all-reduce.3
  170.8 82.2 all-reduce.5
  257.1 69.0 reduce-scatter.6
  329.2 45.7 all-reduce.7
  378.5 73.1 reduce-scatter.4
where the time goes:
time: 460 us
  waiting for transfers between devices  390 us (85%)
  matrix products  39.8 us (9%)
  between operations  13.9 us (3%)
  other arithmetic  11.6 us (3%)
    psum x1, waiting for transfers between devices, local(): lax.psum(jnp.concatenate([gate_preactivation, up_preactivation, returned_...  136 us
    reduce_scatter x1, waiting for transfers between devices, local(): lax.psum_scatter(ffn_part, 'head', scatter_dimension=0, tiled=True)  73.9 us
    unnamed x6, waiting for transfers between devices  71.5 us
    psum x1, waiting for transfers between devices, local(): lax.psum(shared_term.astype(jnp.bfloat16), ('dp', 'head'))  61.1 us
    psum x1, waiting for transfers between devices, local(): lax.psum(head_contributions.reshape(local_heads, reduced_activation, d_co...  48 us
    dot_general x5, matrix products, contract_last(): lax.dot_general(left, right, (((1,), (1,)), ((), ())), preferred_element_...  24.4 us
  transfers between devices with their start and end apart: 5, of which 5 were waited for; matrix products, arithmetic and copies ran while one was open for 6% of the time, Pallas kernels for 0%

commit v1 on v0

--- a/solution.py
+++ b/solution.py
@@ -82,9 +82,14 @@
     head_contributions = ADAPTER_SCALE * lax.dot_general(
         selector_mask, cotangent, (((0,), (0,)), ((), ())), preferred_element_type=jnp.float32
     )
-    up_head_gradients = lax.psum(
-        head_contributions.reshape(local_heads, reduced_activation, d_cols).astype(jnp.bfloat16),
-        "dp",
+    up_head_gradients = jnp.sum(
+        lax.all_gather(
+            head_contributions.reshape(local_heads, reduced_activation, d_cols).astype(
+                jnp.bfloat16
+            ),
+            "dp",
+        ),
+        axis=0,
     ).astype(jnp.float32)
     shared_term = lax.dot_general(
         tokens, selector_gradient, (((0,), (0,)), ((), ())), preferred_element_type=jnp.float32

time: 460 us -> 448 us (0.974)
  waiting for transfers between devices: 390 us -> 378 us
    psum x1 -> x0, waiting for transfers between devices: 48 us -> none  [local(): lax.psum(head_contributions.reshape(local_heads, reduced_activation, d_co...]
    all_gather x0 -> x1, waiting for transfers between devices: none -> 36.1 us  [local(): lax.all_gather(head_contributions.reshape(local_heads, reduced_activation...]
where the time goes in v1:
time: 448 us
  waiting for transfers between devices  378 us (84%)
  matrix products  39 us (9%)
  between operations  13.9 us (3%)
  other arithmetic  12.5 us (3%)
    psum x1, waiting for transfers between devices, local(): lax.psum(jnp.concatenate([gate_preactivation, up_preactivation, returned_...  136 us
    reduce_scatter x1, waiting for transfers between devices, local(): lax.psum_scatter(ffn_part, 'head', scatter_dimension=0, tiled=True)  73.3 us
    unnamed x6, waiting for transfers between devices  71.5 us
    psum x1, waiting for transfers between devices, local(): lax.psum(shared_term.astype(jnp.bfloat16), ('dp', 'head'))  61.2 us
    all_gather x1, waiting for transfers between devices, local(): lax.all_gather(head_contributions.reshape(local_heads, reduced_activation...  36.1 us
    dot_general x5, matrix products, contract_last(): lax.dot_general(left, right, (((1,), (1,)), ((), ())), preferred_element_...  24.2 us
  transfers between devices with their start and end apart: 5, of which 5 were waited for; matrix products, arithmetic and copies ran while one was open for 6% of the time, Pallas kernels for 0%

profile of v1, /device:TPU:0, one launch (start us, length us, event | category | flops | bytes accessed | tf_op | source)
XLA Modules:
  0.0 447.8 jit_solution(8860323344245272787)
XLA Ops:
  7.2 0.8 fusion.15
  8.1 7.5 %convolution_dynamic-update-slice_fusion.2 = f32[256,11216]{0,1:T(8,128)} fusion(bf16[256,1024]{1,0:T(8,128)(2,1)} %param.8, bf16[1024,3696]{0,1:T(8,128)(2,1)} %param.10), kind=kOutput, calls=%fused_computation.2 | convolution fusion | flops 1937768448 | bytes 11878400 | tf_op jit(solution)/shard_map/dot_general | solution.py:25
  15.6 4.1 convolution_dynamic-update-slice_fusion.1
  20.3 4.1 convolution_dynamic-update-slice_fusion
  24.4 0.9 convolution_dynamic-update-slice_fusion.3
  25.3 0.6 multiply_dynamic-update-slice_fusion
  26.0 135.7 %all-reduce.3.cloned.1.call-done = f32[256,11216]{0,1:T(8,128)} async-done(((f32[256,11216]{0,1:T(8,128)}), f32[256,11216]{0,1:T(8,128)}) %all-reduce.3.cloned.1.call-update) | async-done | bytes 11485200 | tf_op jit(solution)/shard_map/psum | solution.py:33
  161.8 4.8 %convert.5 = bf16[256,11216]{0,1:T(8,128)(2,1)S(1)} convert(f32[256,11216]{0,1:T(8,128)} %all-reduce.3.cloned.1.call-done) | non-fusion elementwise | flops 2871296 | bytes 17227776 | tf_op jit(solution)/shard_map/convert.2
  166.6 2.4 copy-done.1
  169.0 0.9 fusion.10
  170.0 0.8 fusion.18
  170.8 0.8 copy.13
  171.6 1.4 multiply_convert_fusion.1
  173.3 7.7 %fusion.3 = f32[256,1024]{1,0:T(8,128)S(1)} fusion(bf16[1024,3696]{0,1:T(8,128)(2,1)} %param.11, f32[256,11216]{0,1:T(8,128)} %all-reduce.3.cloned.1.call-done), kind=kOutput, calls=%fused_computation.10 | convolution fusion | flops 1943445504 | bytes 16187392 | tf_op jit(solution)/shard_map/dot_general | solution.py:10
  181.0 10.2 %fusion.6 = f32[256,1024]{1,0:T(8,128)} fusion(f32[256,1024]{1,0:T(8,128)S(1)} %fusion.3, bf16[1024,3696]{0,1:T(8,128)(2,1)} %param.10, f32[256,11216]{0,1:T(8,128)} %all-reduce.3.cloned.1.call-done), kind=kOutput, calls=%fused_computation.12 | convolution fusion | flops 1947492352 | bytes 21020672 | tf_op jit(solution)/shard_map/dot_general | solution.py:10
  191.2 61.2 %all-reduce.5.cloned.1.call-done = bf16[1024,64]{0,1:T(8,128)(2,1)} async-done(((bf16[1024,64]{0,1:T(8,128)(2,1)}), bf16[1024,64]{0,1:T(8,128)(2,1)}) %all-reduce.5.cloned.1.call-update) | async-done | bytes 131088 | tf_op jit(solution)/shard_map/psum | solution.py:97
  252.4 1.6 convert_element_type.70
  254.0 71.5 %reduce-scatter.7.cloned.1.call-done = f32[32,64]{1,0:T(8,128)} async-done(((f32[256,64]{1,0:T(8,128)}), f32[32,64]{1,0:T(8,128)}) %reduce-scatter.7.cloned.1.call-update) | async-done | bytes 8208
  325.4 0.8 copy.14
  326.3 36.1 %all-gather.2.cloned.1.call-done = bf16[2,8,64,1024]{3,2,1,0:T(8,128)(2,1)} async-done(((bf16[1,8,64,1024]{3,2,1,0:T(8,128)(2,1)}), bf16[2,8,64,1024]{3,2,1,0:T(8,128)(2,1)}) %all-gather.2.cloned.1.call-update) | async-done | bytes 2097168 | tf_op jit(solution)/shard_map/all_gather | solution.py:86
  362.4 2.2 reduce_sum.22
  364.6 1.6 convert_element_type.74
  366.2 73.3 %reduce-scatter.5.cloned.1.call-done = f32[32,1024]{1,0:T(8,128)} async-done(((f32[256,1024]{1,0:T(8,128)}), f32[32,1024]{1,0:T(8,128)}) %reduce-scatter.5.cloned.1.call-update) | async-done | bytes 131088 | tf_op jit(solution)/shard_map/reduce_scatter | solution.py:71
  439.5 1.7 fusion.11
  (29 shorter events, 1.0 us)
Async XLA Ops:
  7.2 12.6 %copy-start = (bf16[8,64,1024]{2,1,0:T(8,128)(2,1)S(1)}, bf16[8,64,1024]{2,1,0:T(8,128)(2,1)}, u32[]{:S(2)}) copy-start(bf16[8,64,1024]{2,1,0:T(8,128)(2,1)} %param.14) | copy-start | bytes 3145732
  7.2 154.6 %all-reduce.3.cloned.1.call-start = ((), (), s32[]{:S(2)}) async-start(), calls=%async_computation.2 | async-start | bytes 22970368 | tf_op jit(solution)/shard_map/psum | solution.py:33
  8.1 7.5 %copy-start.2 = (bf16[256,1024]{1,0:T(8,128)(2,1)S(1)}, bf16[256,1024]{1,0:T(8,128)(2,1)}, u32[]{:S(2)}) copy-start(bf16[256,1024]{1,0:T(8,128)(2,1)} %param.8) | copy-start | bytes 1572868
  8.1 7.5 %copy-start.5 = (bf16[1024,3696]{0,1:T(8,128)(2,1)S(1)}, bf16[1024,3696]{0,1:T(8,128)(2,1)}, u32[]{:S(2)}) copy-start(bf16[1024,3696]{0,1:T(8,128)(2,1)} %param.11) | copy-start | bytes 22708228
  8.1 12.2 %slice-start = ((s8[7569408]{0:T(1024)(128)(4,1)}), s8[4194304]{0:T(1024)(128)(4,1)S(1)}, s32[]{:S(2)}) async-start(s8[7569408]{0:T(1024)(128)(4,1)} %bitcast.28), calls=%async_computation.7 | async-start | bytes 8388608
  15.6 4.1 copy-start.3
  15.6 4.6 %slice-start.1 = ((s8[7569408]{0:T(1024)(128)(4,1)}), s8[3375104]{0:T(1024)(128)(4,1)S(1)}, s32[]{:S(2)}) async-start(s8[7569408]{0:T(1024)(128)(4,1)} %bitcast.28), calls=%async_computation.8 | async-start | bytes 6750208
  20.3 4.2 copy-start.4
  26.0 226.4 %all-reduce.5.cloned.1.call-start = ((), (), s32[]{:S(2)}) async-start(), calls=%async_computation.4 | async-start | bytes 262144 | tf_op jit(solution)/shard_map/psum | solution.py:97
  166.6 2.5 copy-start.1
  169.9 155.5 %reduce-scatter.7.cloned.1.call-start = ((), (), s32[]{:S(2)}) async-start(), calls=%async_computation.6 | async-start | bytes 147456
  171.5 190.8 %all-gather.2.cloned.1.call-start = ((), (), s32[]{:S(2)}) async-start(), calls=%async_computation.5 | async-start | bytes 3145728 | tf_op jit(solution)/shard_map/all_gather | solution.py:86
  173.1 266.4 %reduce-scatter.5.cloned.1.call-start = ((), (), s32[]{:S(2)}) async-start(), calls=%async_computation.3 | async-start | bytes 1179648 | tf_op jit(solution)/shard_map/reduce_scatter | solution.py:71
Sparse Core Ops, SparseCore 0:
  26.1 135.6 all-reduce.2
  170.1 82.2 all-reduce.4
  256.3 69.0 reduce-scatter.6
  327.6 34.6 all-gather.1
  366.3 73.1 reduce-scatter.4
